TPU v7x, 512 devices: a whole 4x8x8 slice. The times are simulated.
512 devices in a mesh: dp: 16 (over y_hi, x, core), seq: 32 (over z, y_lo).
Axes of the slice: x: 4, y: 8 (y_hi: 2, y_lo: 4; y = y_hi * 4 + y_lo), z: 8, core: 2. Of those that a mesh axis runs over, the one named last changes fastest.
Arguments:
- pre_gate: bfloat16 [16, 4096, 2048], P('dp', 'seq'), may hold values from -6 to 6
- post_gate: bfloat16 [16, 4096, 2048], P('dp', 'seq'), may hold values from -6 to 6
- values: bfloat16 [16, 4096, 2048], P('dp', 'seq'), may hold values from -6 to 6
- cotangent: bfloat16 [16, 4096, 2048], P('dp', 'seq'), may hold values from -6 to 6
- filters: bfloat16 [1024, 16], P(('dp', 'seq')), may hold values from -0.1875 to 0.1875
Outputs:
- output: bfloat16 [16, 4096, 2048], P('dp', 'seq')
- grad_pre: bfloat16 [16, 4096, 2048], P('dp', 'seq')
- grad_post: bfloat16 [16, 4096, 2048], P('dp', 'seq')
- grad_values: bfloat16 [16, 4096, 2048], P('dp', 'seq')
- grad_filters: float32 [1024, 16], P(('dp', 'seq'))
All inputs are finite; a program needn't handle non-finite values.
Results may differ from a plain program's by a relative error of at most 0.005.
Values may be sent and summed in bfloat16 or wider, within the bound.
A program may use at most 128 MiB of HBM per device.

v0:
```python
import jax
import jax.numpy as jnp
import numpy as np
from jax import lax
from jax.sharding import PartitionSpec as P

K = 1024


def shifted(value, axis, steps):
    count = lax.axis_size(axis)
    first, last = (max(0, -steps), min(count, count - steps))
    return lax.ppermute(value, axis, [(source, source + steps) for source in range(first, last)])


def tile_index(lag_blocks, shard_len):
    offsets = np.arange(lag_blocks)[:, None, None] * shard_len
    rows_idx = np.arange(shard_len)[None, :, None]
    cols_idx = np.arange(shard_len)[None, None, :]
    return (offsets + rows_idx - cols_idx + shard_len).astype(np.int32)


def build_tiles(all_taps, lag_blocks, shard_len):
    tap_count = all_taps.shape[0]
    needed = (lag_blocks + 1) * shard_len
    trailing = max(needed - shard_len - tap_count, 0)
    padded = jnp.concatenate(
        [
            jnp.zeros((shard_len, all_taps.shape[1]), all_taps.dtype),
            all_taps,
            jnp.zeros((trailing, all_taps.shape[1]), all_taps.dtype),
        ],
        axis=0,
    )
    columns = padded.T
    return columns[:, tile_index(lag_blocks, shard_len)]


def earlier_relay(piece_in, history_len):

    def earlier_advance(moving, unused):
        arrived = shifted(moving, "seq", 1)
        return (arrived, arrived)

    unused_last, stacked = lax.scan(earlier_advance, piece_in, None, length=history_len)
    return jnp.concatenate([piece_in[None], stacked], axis=0)


def later_relay(piece_in, history_len):

    def later_advance(moving, unused):
        arrived = shifted(moving, "seq", -1)
        return (arrived, arrived)

    unused_last, stacked = lax.scan(later_advance, piece_in, None, length=history_len)
    return jnp.concatenate([piece_in[None], stacked], axis=0)


def lag_window(gated_rows, history, local_groups, group_width, lag_count):
    row_count = gated_rows.shape[0]
    span_len = history.shape[0]
    front_zero = jnp.zeros((row_count, history.shape[1]), history.dtype)
    widened = jnp.concatenate([front_zero, history], axis=0)
    gated_grp = gated_rows.reshape(row_count, local_groups, group_width).transpose(1, 0, 2)
    hist_grp = widened.reshape(span_len + row_count, local_groups, group_width).transpose(1, 0, 2)

    def one_group(pair_in):
        gated_one, hist_one = pair_in
        product = lax.dot_general(
            gated_one, hist_one, (((1,), (1,)), ((), ())), preferred_element_type=jnp.float32
        )
        padded = jnp.pad(product, ((0, 0), (0, row_count)))
        flat_line = jnp.concatenate(
            [padded.reshape(-1), jnp.zeros((row_count,), jnp.float32)], axis=0
        )
        skewed = flat_line.reshape(row_count, span_len + 2 * row_count + 1)
        diag_sums = jnp.sum(skewed, axis=0)
        return jnp.flip(diag_sums[1 : span_len + 1], axis=0)[:lag_count]

    return lax.map(one_group, (gated_grp, hist_grp))


def shards(pre_gate, post_gate, values, cotangent, filters):
    shard_len = pre_gate.shape[1]
    channels = pre_gate.shape[2]
    groups = filters.shape[1]
    group_size = channels // groups
    seq_count = lax.axis_size("seq")
    all_taps = lax.all_gather(filters, ("dp", "seq"), axis=0, tiled=True)
    mixed_in = (pre_gate[0].astype(jnp.float32) * values[0]).astype(jnp.bfloat16)
    gated = (cotangent[0].astype(jnp.float32) * post_gate[0]).astype(jnp.bfloat16)
    history_len = min(-(-K // shard_len), seq_count - 1)
    lag_blocks = history_len + 1
    mixed_ext = earlier_relay(mixed_in, history_len)
    gated_ext = later_relay(gated, history_len)
    mixed_four = mixed_ext.reshape(lag_blocks, shard_len, groups, group_size)
    gated_four = gated_ext.reshape(lag_blocks, shard_len, groups, group_size)
    tiles = build_tiles(all_taps, lag_blocks, shard_len)
    convolved = jnp.einsum(
        "gmij,mjgc->igc", tiles, mixed_four, preferred_element_type=jnp.float32
    ).reshape(shard_len, channels)
    carried = jnp.einsum(
        "gmji,mjgc->igc", tiles, gated_four, preferred_element_type=jnp.float32
    ).reshape(shard_len, channels)
    hist_len = lag_blocks * shard_len
    lag_count = min(K, hist_len)
    history = jnp.flip(mixed_ext, axis=0).reshape(hist_len, channels)
    lag_local = lag_window(gated, history, groups, group_size, lag_count)
    partial_grads = lag_local.T
    output = (post_gate[0].astype(jnp.float32) * convolved).astype(jnp.bfloat16)
    grad_post = (cotangent[0].astype(jnp.float32) * convolved).astype(jnp.bfloat16)
    grad_pre = (carried * values[0]).astype(jnp.bfloat16)
    grad_values = (carried * pre_gate[0]).astype(jnp.bfloat16)
    owned = lax.psum_scatter(partial_grads, ("dp", "seq"), scatter_dimension=0, tiled=True)
    total_tokens = lax.axis_size("dp") * shard_len * seq_count * group_size
    grad_filters = owned / float(total_tokens**0.5)
    return (output[None], grad_pre[None], grad_post[None], grad_values[None], grad_filters)


def solution(mesh):
    return jax.shard_map(
        shards,
        mesh=mesh,
        in_specs=(
            P("dp", "seq", None),
            P("dp", "seq", None),
            P("dp", "seq", None),
            P("dp", "seq", None),
            P(("dp", "seq"), None),
        ),
        out_specs=(
            P("dp", "seq", None),
            P("dp", "seq", None),
            P("dp", "seq", None),
            P("dp", "seq", None),
            P(("dp", "seq"), None),
        ),
        check_vma=False,
    )
```

profile of v0, /device:TPU:24, one launch (start us, length us, event | category | flops | bytes accessed | tf_op | source)
XLA Modules:
  0.0 2391.0 jit_solution(9912820649971849793)
XLA Ops:
  7.2 1.3 fusion.20
  9.6 1234.1 %all-gather = bf16[512,2,16]{2,1,0:T(2,128)(2,1)S(1)} all-gather(bf16[1,2,16]{2,1,0:T(2,128)(2,1)} %bitcast.77), channel_id=1, replica_groups=mesh['dp'=16,'seq'=32] {'dp','seq'}, dimensions={0}, use_global_device_ids=true | all-gather | bytes 32832 | tf_op jit(solution)/shard_map/all_gather | solution.py:89
  1244.9 510.5 %gather_fusion = bf16[147456,16]{1,0:T(8,128)(2,1)} fusion(bf16[16,1280]{0,1:T(8,128)(2,1)S(1)} %maximum_bitcast_fusion, s32[147456]{0:T(1024)S(1)} %broadcast_clamp_fusion), kind=kCustom, calls=%fused_computation | custom fusion | bytes 10027008 | tf_op jit(solution)/shard_map/gather | solution.py:36
  1755.4 30.3 %copy.71 = bf16[9,128,128,16]{2,1,0,3:T(8,128)(2,1)} copy(bf16[9,128,128,16]{3,2,1,0:T(8,128)(2,1)} %bitcast.61) | data formatting | bytes 9437184 | tf_op jit(solution)/shard_map/gather | solution.py:36
  1785.8 150.7 %while.37 = (s32[]{:T(128)}, bf16[128,2048]{1,0:T(8,128)(2,1)S(1)}, bf16[8,128,2048]{1,2,0:T(8,128)(2,1)}, s32[]{:T(128)}) while((s32[]{:T(128)}, bf16[128,2048]{1,0:T(8,128)(2,1)S(1)}, bf16[8,128,2048]{1,2,0:T(8,128)(2,1)}, s32[]{:T(128)}) %tuple.63), condition=%wide.region_3.4_spmd, body=%wide.region_2.3_spmd.sunk | while | flops 2 | bytes 5242985 | solution.py:55
  1785.9 7.8 collective-permute-start.1
  1793.6 11.7 collective-permute-done.1
  1806.5 4.4 collective-permute-start.1
  1810.9 14.7 collective-permute-done.1
  1826.8 1.9 collective-permute-start.1
  1828.8 16.3 collective-permute-done.1
  1846.2 1.9 collective-permute-start.1
  1848.2 16.3 collective-permute-done.1
  1865.6 1.9 collective-permute-start.1
  1867.5 14.7 collective-permute-done.1
  1883.4 1.9 collective-permute-start.1
  1885.3 14.6 collective-permute-done.1
  1901.1 1.9 collective-permute-start.1
  1903.0 14.6 collective-permute-done.1
  1918.8 1.9 collective-permute-start.1
  1920.7 14.7 collective-permute-done.1
  1936.6 5.2 fusion.10
  1942.1 2.3 fusion.17
  1944.8 115.4 %while.36 = (s32[]{:T(128)}, bf16[128,2048]{1,0:T(8,128)(2,1)S(1)}, bf16[8,128,2048]{2,1,0:T(8,128)(2,1)}, s32[]{:T(128)}) while((s32[]{:T(128)}, bf16[128,2048]{1,0:T(8,128)(2,1)S(1)}, bf16[8,128,2048]{2,1,0:T(8,128)(2,1)}, s32[]{:T(128)}) %tuple.66), condition=%wide.region_1.2_spmd, body=%wide.region_0.1_spmd.sunk | while | flops 2 | bytes 4194409 | solution.py:45
  1944.8 1.9 collective-permute-start
  1946.7 12.9 collective-permute-done
  1960.5 1.9 collective-permute-start
  1962.4 14.1 collective-permute-done
  1977.5 1.9 collective-permute-start
  1979.4 9.1 collective-permute-done
  1989.4 4.6 collective-permute-start
  1994.0 6.7 collective-permute-done
  2001.6 7.1 collective-permute-start
  2008.7 6.7 collective-permute-done
  2016.3 7.1 collective-permute-start
  2023.3 6.7 collective-permute-done
  2030.9 7.1 collective-permute-start
  2038.0 6.7 collective-permute-done
  2045.5 7.1 collective-permute-start
  2052.6 6.7 collective-permute-done
  2060.2 4.8 pad_maximum_fusion
  2064.9 5.2 rev.6
  2070.1 6.8 copy.89
  2076.9 5.0 concatenate.35.clone
  2081.9 34.4 %while.38 = (s32[]{:T(128)}, f32[16,1024]{1,0:T(8,128)S(1)}, bf16[16,128,128]{2,1,0:T(8,128)(2,1)S(1)}, bf16[16,1280,128]{1,2,0:T(8,128)(2,1)}, s32[]{:T(128)}, /*index=5*/f32[]{:T(128)}, s32[]{:T(128)}) while((s32[]{:T(128)}, f32[16,1024]{1,0:T(8,128)S(1)}, bf16[16,128,128]{2,1,0:T(8,128)(2,1)S(1)}, bf16[16,1280,128]{1,2,0:T(8,128)(2,1)}, ...), condition=%wide.region_6.7_spmd, body=%wide.region_4.6_spmd.sunk | while | flops 42121984 | bytes 7471721 | solution.py:80
  2084.0 1.2 fusion.31
  2086.2 1.2 fusion.31
  2088.3 1.2 fusion.31
  2090.5 1.2 fusion.31
  2092.6 1.2 fusion.31
  2094.8 1.2 fusion.31
  2096.9 1.2 fusion.31
  2099.1 1.2 fusion.31
  2101.3 1.2 fusion.31
  2103.4 1.2 fusion.31
  2105.6 1.2 fusion.31
  2107.7 1.2 fusion.31
  2109.9 1.2 fusion.31
  2112.0 1.2 fusion.31
  2117.6 6.4 copy.69
  2124.1 5.4 fusion.6
  2129.8 1.2 fusion.21
  2131.0 251.9 %all-reduce.6.cloned.1.call-done = f32[1024,16]{1,0:T(8,128)} async-done(((f32[1024,16]{1,0:T(8,128)}), f32[1024,16]{1,0:T(8,128)}) %all-reduce.6.cloned.1.call-update) | async-done | bytes 65552
  2382.9 1.2 dynamic-slice_multiply_fusion
  (193 shorter events, 37.3 us)
Async XLA Ops:
  7.2 2375.7 %all-reduce.6.cloned.1.call-start = ((), (), s32[]{:S(2)}) async-start(), calls=%async_computation | async-start | bytes 1048576
  1785.9 19.5 collective-permute-start.1
  1806.5 19.1 collective-permute-start.1
  1826.8 18.2 collective-permute-start.1
  1846.2 18.2 collective-permute-start.1
  1865.6 16.6 collective-permute-start.1
  1883.4 16.5 collective-permute-start.1
  1901.1 16.6 collective-permute-start.1
  1918.8 16.6 collective-permute-start.1
  1936.6 5.6 copy-start.2
  1944.8 14.8 collective-permute-start
  1960.5 16.1 collective-permute-start
  1977.5 11.1 collective-permute-start
  1989.4 11.3 collective-permute-start
  2001.6 13.8 collective-permute-start
  2016.3 13.8 collective-permute-start
  2030.9 13.8 collective-permute-start
  2045.5 13.8 collective-permute-start
  2124.1 5.7 copy-start
  2124.1 5.7 copy-start.1
Sparse Core Ops, SparseCore 0:
  2117.5 265.3 all-reduce.5
where the time goes:
time: 2390 us
  blocking collectives  1230 us (51%)
  local copies, waits for them, and re-layouts  597 us (25%)
  waiting for transfers between devices  439 us (18%)
  starting transfers between devices  62.3 us (3%)
  matrix products  29.8 us (1%)
    all_gather x1, blocking collectives, shards(): all_taps = lax.all_gather(filters, ('dp', 'seq'), axis=0, tiled=True)  1230 us
    gather x2, local copies, waits for them, and re-layouts, build_tiles(): return columns[:, tile_index(lag_blocks, shard_len)]  541 us
    unnamed x2, waiting for transfers between devices  252 us
    ppermute x16, waiting for transfers between devices, shifted(): lax.ppermute(value, axis, [(source, source + steps) for source in range(f...  187 us
    ppermute x16, starting transfers between devices, shifted(): lax.ppermute(value, axis, [(source, source + steps) for source in range(f...  62.3 us
  transfers between devices with their start and end apart: 17, of which 17 were waited for; matrix products, arithmetic and copies ran while one was open for 1% of the time, Pallas kernels for 0%

commit v1 on v0

--- a/solution.py
+++ b/solution.py
@@ -86,7 +86,8 @@
     groups = filters.shape[1]
     group_size = channels // groups
     seq_count = lax.axis_size("seq")
-    all_taps = lax.all_gather(filters, ("dp", "seq"), axis=0, tiled=True)
+    sent = jnp.stack([filters] * lax.axis_size(("dp", "seq")))
+    all_taps = jnp.concatenate(lax.all_to_all(sent, ("dp", "seq"), 0, 0), axis=0)
     mixed_in = (pre_gate[0].astype(jnp.float32) * values[0]).astype(jnp.bfloat16)
     gated = (cotangent[0].astype(jnp.float32) * post_gate[0]).astype(jnp.bfloat16)
     history_len = min(-(-K // shard_len), seq_count - 1)

time: 2390 us -> 1240 us (0.52)
  blocking collectives: 1230 us -> 0 us
  waiting for transfers between devices: 439 us -> 503 us
    all_gather x1 -> x0, blocking collectives: 1230 us -> none  [shards(): all_taps = lax.all_gather(filters, ('dp', 'seq'), axis=0, tiled=True)]
    unnamed x2, waiting for transfers between devices: 252 us -> 292 us
  transfers between devices with their start and end apart: 17 -> 18, of which waited for: 17 -> 18; matrix products, arithmetic and copies ran while one was open for 1% -> 1% of each run, Pallas kernels for 0% -> 0%
where the time goes in v1:
time: 1240 us
  local copies, waits for them, and re-layouts  604 us (49%)
  waiting for transfers between devices  503 us (41%)
  starting transfers between devices  73.5 us (6%)
  matrix products  26.4 us (2%)
  between operations  14.2 us (1%)
  other arithmetic  13.6 us (1%)
    gather x2, local copies, waits for them, and re-layouts, build_tiles(): return columns[:, tile_index(lag_blocks, shard_len)]  544 us
    unnamed x2, waiting for transfers between devices  292 us
    ppermute x16, waiting for transfers between devices, shifted(): lax.ppermute(value, axis, [(source, source + steps) for source in range(f...  201 us
    ppermute x16, starting transfers between devices, shifted(): lax.ppermute(value, axis, [(source, source + steps) for source in range(f...  52.6 us
  transfers between devices with their start and end apart: 18, of which 18 were waited for; matrix products, arithmetic and copies ran while one was open for 1% of the time, Pallas kernels for 0%

profile of v1, /device:TPU:24, one launch (start us, length us, event | category | flops | bytes accessed | tf_op | source)
XLA Modules:
  0.0 1237.0 jit_solution(5882294043281908754)
XLA Ops:
  7.2 1.5 stack.2
  8.7 20.9 %all-to-all-start = ((bf16[512,2,16]{2,1,0:T(2,128)(2,1)}), bf16[512,2,16]{2,1,0:T(2,128)(2,1)S(1)}, u32[]{:S(2)}, u32[]{:S(2)}) async-start(bf16[512,2,16]{2,1,0:T(2,128)(2,1)} %stack.2), calls=%async_computation | async-start | bytes 524288 | tf_op jit(solution)/shard_map/all_to_all | solution.py:90
  30.8 1.3 fusion.20
  34.2 10.2 all-to-all-done
  44.5 514.1 %gather_fusion = bf16[147456,16]{1,0:T(8,128)(2,1)} fusion(bf16[16,1280]{0,1:T(8,128)(2,1)S(1)} %maximum_bitcast_fusion, s32[147456]{0:T(1024)S(1)} %broadcast_clamp_fusion), kind=kCustom, calls=%fused_computation | custom fusion | bytes 10027008 | tf_op jit(solution)/shard_map/gather | solution.py:36
  558.5 30.4 %copy.88 = bf16[9,128,128,16]{2,1,0,3:T(8,128)(2,1)} copy(bf16[9,128,128,16]{3,2,1,0:T(8,128)(2,1)} %bitcast.60) | data formatting | bytes 9437184 | tf_op jit(solution)/shard_map/gather | solution.py:36
  588.9 133.2 %while.37 = (s32[]{:T(128)}, bf16[128,2048]{1,0:T(8,128)(2,1)S(1)}, bf16[8,128,2048]{1,2,0:T(8,128)(2,1)}, s32[]{:T(128)}) while((s32[]{:T(128)}, bf16[128,2048]{1,0:T(8,128)(2,1)S(1)}, bf16[8,128,2048]{1,2,0:T(8,128)(2,1)}, s32[]{:T(128)}) %tuple.76), condition=%wide.region_3.4_spmd, body=%wide.region_2.3_spmd.sunk | while | flops 2 | bytes 5242985 | solution.py:55
  588.9 3.2 collective-permute-start.1
  592.1 15.2 %collective-permute-done.1 = bf16[128,2048]{1,0:T(8,128)(2,1)S(1)} collective-permute-done((bf16[128,2048]{1,0:T(8,128)(2,1)S(1)}, bf16[128,2048]{1,0:T(8,128)(2,1)S(1)}, u32[]{:S(2)}, u32[]{:S(2)}) %collective-permute-start.1) | collective-permute-done | bytes 524320 | tf_op jit(solution)/shard_map/while/body/eval_jaxpr/ppermute | solution.py:13
  608.5 1.9 collective-permute-start.1
  610.4 15.5 %collective-permute-done.1 = bf16[128,2048]{1,0:T(8,128)(2,1)S(1)} collective-permute-done((bf16[128,2048]{1,0:T(8,128)(2,1)S(1)}, bf16[128,2048]{1,0:T(8,128)(2,1)S(1)}, u32[]{:S(2)}, u32[]{:S(2)}) %collective-permute-start.1) | collective-permute-done | bytes 524320 | tf_op jit(solution)/shard_map/while/body/eval_jaxpr/ppermute | solution.py:13
  627.1 1.9 collective-permute-start.1
  629.0 14.5 %collective-permute-done.1 = bf16[128,2048]{1,0:T(8,128)(2,1)S(1)} collective-permute-done((bf16[128,2048]{1,0:T(8,128)(2,1)S(1)}, bf16[128,2048]{1,0:T(8,128)(2,1)S(1)}, u32[]{:S(2)}, u32[]{:S(2)}) %collective-permute-start.1) | collective-permute-done | bytes 524320 | tf_op jit(solution)/shard_map/while/body/eval_jaxpr/ppermute | solution.py:13
  644.7 1.9 collective-permute-start.1
  646.7 13.6 %collective-permute-done.1 = bf16[128,2048]{1,0:T(8,128)(2,1)S(1)} collective-permute-done((bf16[128,2048]{1,0:T(8,128)(2,1)S(1)}, bf16[128,2048]{1,0:T(8,128)(2,1)S(1)}, u32[]{:S(2)}, u32[]{:S(2)}) %collective-permute-start.1) | collective-permute-done | bytes 524320 | tf_op jit(solution)/shard_map/while/body/eval_jaxpr/ppermute | solution.py:13
  661.5 1.9 collective-permute-start.1
  663.4 12.7 %collective-permute-done.1 = bf16[128,2048]{1,0:T(8,128)(2,1)S(1)} collective-permute-done((bf16[128,2048]{1,0:T(8,128)(2,1)S(1)}, bf16[128,2048]{1,0:T(8,128)(2,1)S(1)}, u32[]{:S(2)}, u32[]{:S(2)}) %collective-permute-start.1) | collective-permute-done | bytes 524320 | tf_op jit(solution)/shard_map/while/body/eval_jaxpr/ppermute | solution.py:13
  677.3 1.9 collective-permute-start.1
  679.2 11.8 collective-permute-done.1
  692.3 1.9 collective-permute-start.1
  694.2 11.8 collective-permute-done.1
  707.2 1.9 collective-permute-start.1
  709.1 11.8 collective-permute-done.1
  722.2 5.1 fusion.10
  727.6 1.3 fusion.17
  729.2 137.6 %while.36 = (s32[]{:T(128)}, bf16[128,2048]{1,0:T(8,128)(2,1)S(1)}, bf16[8,128,2048]{2,1,0:T(8,128)(2,1)}, s32[]{:T(128)}) while((s32[]{:T(128)}, bf16[128,2048]{1,0:T(8,128)(2,1)S(1)}, bf16[8,128,2048]{2,1,0:T(8,128)(2,1)}, s32[]{:T(128)}) %tuple.67), condition=%wide.region_1.2_spmd, body=%wide.region_0.1_spmd.sunk | while | flops 2 | bytes 4194409 | solution.py:45
  729.2 1.9 collective-permute-start
  731.2 13.0 %collective-permute-done = bf16[128,2048]{1,0:T(8,128)(2,1)S(1)} collective-permute-done((bf16[128,2048]{1,0:T(8,128)(2,1)S(1)}, bf16[128,2048]{1,0:T(8,128)(2,1)S(1)}, u32[]{:S(2)}, u32[]{:S(2)}) %collective-permute-start) | collective-permute-done | bytes 524320 | tf_op jit(solution)/shard_map/while/body/eval_jaxpr/ppermute | solution.py:13
  745.1 1.9 collective-permute-start
  747.0 14.2 %collective-permute-done = bf16[128,2048]{1,0:T(8,128)(2,1)S(1)} collective-permute-done((bf16[128,2048]{1,0:T(8,128)(2,1)S(1)}, bf16[128,2048]{1,0:T(8,128)(2,1)S(1)}, u32[]{:S(2)}, u32[]{:S(2)}) %collective-permute-start) | collective-permute-done | bytes 524320 | tf_op jit(solution)/shard_map/while/body/eval_jaxpr/ppermute | solution.py:13
  762.1 1.9 collective-permute-start
  764.0 14.2 %collective-permute-done = bf16[128,2048]{1,0:T(8,128)(2,1)S(1)} collective-permute-done((bf16[128,2048]{1,0:T(8,128)(2,1)S(1)}, bf16[128,2048]{1,0:T(8,128)(2,1)S(1)}, u32[]{:S(2)}, u32[]{:S(2)}) %collective-permute-start) | collective-permute-done | bytes 524320 | tf_op jit(solution)/shard_map/while/body/eval_jaxpr/ppermute | solution.py:13
  779.2 3.0 collective-permute-start
  782.1 12.4 collective-permute-done
  795.4 6.0 collective-permute-start
  801.4 12.2 collective-permute-done
  814.4 7.1 collective-permute-start
  821.5 11.3 collective-permute-done
  833.7 7.1 collective-permute-start
  840.8 10.4 collective-permute-done
  852.1 7.1 collective-permute-start
  859.2 6.7 collective-permute-done
  866.8 6.5 copy.86
  873.3 5.1 pad_maximum_fusion
  878.5 1.3 copy-done
  879.7 1.8 fusion.6
  881.9 5.2 rev.6
  887.1 6.7 copy.106
  893.8 5.0 concatenate.35.clone
  898.8 34.7 %while.38 = (s32[]{:T(128)}, f32[16,1024]{1,0:T(8,128)S(1)}, bf16[16,128,128]{2,1,0:T(8,128)(2,1)}, bf16[16,1280,128]{1,2,0:T(8,128)(2,1)}, s32[]{:T(128)}, /*index=5*/f32[]{:T(128)}, s32[]{:T(128)}) while((s32[]{:T(128)}, f32[16,1024]{1,0:T(8,128)S(1)}, bf16[16,128,128]{2,1,0:T(8,128)(2,1)}, bf16[16,1280,128]{1,2,0:T(8,128)(2,1)}, s32[]{:T(128)}, ...), condition=%wide.region_6.7_spmd, body=%wide.region_4.6_spmd.sunk | while | flops 42121984 | bytes 7471721 | solution.py:80
  901.0 1.2 fusion.31
  903.2 1.2 fusion.31
  905.3 1.2 fusion.31
  907.5 1.2 fusion.31
  909.7 1.2 fusion.31
  911.8 1.2 fusion.31
  914.0 1.2 fusion.31
  916.2 1.2 fusion.31
  918.4 1.2 fusion.31
  924.9 1.2 fusion.31
  929.2 1.2 fusion.31
  934.6 2.5 fusion.21
  937.1 291.9 %all-reduce.6.cloned.1.call-done = f32[1024,16]{1,0:T(8,128)} async-done(((f32[1024,16]{1,0:T(8,128)}), f32[1024,16]{1,0:T(8,128)}) %all-reduce.6.cloned.1.call-update) | async-done | bytes 65552
  1228.9 1.2 dynamic-slice_multiply_fusion
  (201 shorter events, 41.9 us)
Async XLA Ops:
  8.7 35.7 %all-to-all-start = ((bf16[512,2,16]{2,1,0:T(2,128)(2,1)}), bf16[512,2,16]{2,1,0:T(2,128)(2,1)S(1)}, u32[]{:S(2)}, u32[]{:S(2)}) async-start(bf16[512,2,16]{2,1,0:T(2,128)(2,1)} %stack.2), calls=%async_computation | async-start | bytes 524288 | tf_op jit(solution)/shard_map/all_to_all | solution.py:90
  29.6 1199.3 %all-reduce.6.cloned.1.call-start = ((), (), s32[]{:S(2)}) async-start(), calls=%async_computation.1 | async-start | bytes 1048576
  588.9 133.2 %copy-start.3 = (bf16[1,128,2048]{1,2,0:T(8,128)(2,1)S(1)}, bf16[1,128,2048]{1,2,0:T(8,128)(2,1)}, u32[]{:S(2)}) copy-start(bf16[1,128,2048]{1,2,0:T(8,128)(2,1)} %copy.90) | copy-start | bytes 1572868
  588.9 18.4 %collective-permute-start.1 = (bf16[128,2048]{1,0:T(8,128)(2,1)S(1)}, bf16[128,2048]{1,0:T(8,128)(2,1)S(1)}, u32[]{:S(2)}, u32[]{:S(2)}) collective-permute-start(bf16[128,2048]{1,0:T(8,128)(2,1)S(1)} %get-tuple-element.208), channel_id=1, source_target_pairs={{1,0},{2,1},{3,2},{4,3},{5,4},{6,5},{7,6},{8,7},{9,8},{10,9},{11,1... | collective-permute-start | bytes 1572872 | tf_op jit(solution)/shard_map/while/body/eval_jaxpr/ppermute | solution.py:13
  608.5 17.4 %collective-permute-start.1 = (bf16[128,2048]{1,0:T(8,128)(2,1)S(1)}, bf16[128,2048]{1,0:T(8,128)(2,1)S(1)}, u32[]{:S(2)}, u32[]{:S(2)}) collective-permute-start(bf16[128,2048]{1,0:T(8,128)(2,1)S(1)} %get-tuple-element.208), channel_id=1, source_target_pairs={{1,0},{2,1},{3,2},{4,3},{5,4},{6,5},{7,6},{8,7},{9,8},{10,9},{11,1... | collective-permute-start | bytes 1572872 | tf_op jit(solution)/shard_map/while/body/eval_jaxpr/ppermute | solution.py:13
  627.1 16.5 %collective-permute-start.1 = (bf16[128,2048]{1,0:T(8,128)(2,1)S(1)}, bf16[128,2048]{1,0:T(8,128)(2,1)S(1)}, u32[]{:S(2)}, u32[]{:S(2)}) collective-permute-start(bf16[128,2048]{1,0:T(8,128)(2,1)S(1)} %get-tuple-element.208), channel_id=1, source_target_pairs={{1,0},{2,1},{3,2},{4,3},{5,4},{6,5},{7,6},{8,7},{9,8},{10,9},{11,1... | collective-permute-start | bytes 1572872 | tf_op jit(solution)/shard_map/while/body/eval_jaxpr/ppermute | solution.py:13
  644.7 15.6 %collective-permute-start.1 = (bf16[128,2048]{1,0:T(8,128)(2,1)S(1)}, bf16[128,2048]{1,0:T(8,128)(2,1)S(1)}, u32[]{:S(2)}, u32[]{:S(2)}) collective-permute-start(bf16[128,2048]{1,0:T(8,128)(2,1)S(1)} %get-tuple-element.208), channel_id=1, source_target_pairs={{1,0},{2,1},{3,2},{4,3},{5,4},{6,5},{7,6},{8,7},{9,8},{10,9},{11,1... | collective-permute-start | bytes 1572872 | tf_op jit(solution)/shard_map/while/body/eval_jaxpr/ppermute | solution.py:13
  661.5 14.6 %collective-permute-start.1 = (bf16[128,2048]{1,0:T(8,128)(2,1)S(1)}, bf16[128,2048]{1,0:T(8,128)(2,1)S(1)}, u32[]{:S(2)}, u32[]{:S(2)}) collective-permute-start(bf16[128,2048]{1,0:T(8,128)(2,1)S(1)} %get-tuple-element.208), channel_id=1, source_target_pairs={{1,0},{2,1},{3,2},{4,3},{5,4},{6,5},{7,6},{8,7},{9,8},{10,9},{11,1... | collective-permute-start | bytes 1572872 | tf_op jit(solution)/shard_map/while/body/eval_jaxpr/ppermute | solution.py:13
  677.3 13.8 %collective-permute-start.1 = (bf16[128,2048]{1,0:T(8,128)(2,1)S(1)}, bf16[128,2048]{1,0:T(8,128)(2,1)S(1)}, u32[]{:S(2)}, u32[]{:S(2)}) collective-permute-start(bf16[128,2048]{1,0:T(8,128)(2,1)S(1)} %get-tuple-element.208), channel_id=1, source_target_pairs={{1,0},{2,1},{3,2},{4,3},{5,4},{6,5},{7,6},{8,7},{9,8},{10,9},{11,1... | collective-permute-start | bytes 1572872 | tf_op jit(solution)/shard_map/while/body/eval_jaxpr/ppermute | solution.py:13
  692.3 13.8 %collective-permute-start.1 = (bf16[128,2048]{1,0:T(8,128)(2,1)S(1)}, bf16[128,2048]{1,0:T(8,128)(2,1)S(1)}, u32[]{:S(2)}, u32[]{:S(2)}) collective-permute-start(bf16[128,2048]{1,0:T(8,128)(2,1)S(1)} %get-tuple-element.208), channel_id=1, source_target_pairs={{1,0},{2,1},{3,2},{4,3},{5,4},{6,5},{7,6},{8,7},{9,8},{10,9},{11,1... | collective-permute-start | bytes 1572872 | tf_op jit(solution)/shard_map/while/body/eval_jaxpr/ppermute | solution.py:13
  707.2 13.8 %collective-permute-start.1 = (bf16[128,2048]{1,0:T(8,128)(2,1)S(1)}, bf16[128,2048]{1,0:T(8,128)(2,1)S(1)}, u32[]{:S(2)}, u32[]{:S(2)}) collective-permute-start(bf16[128,2048]{1,0:T(8,128)(2,1)S(1)} %get-tuple-element.208), channel_id=1, source_target_pairs={{1,0},{2,1},{3,2},{4,3},{5,4},{6,5},{7,6},{8,7},{9,8},{10,9},{11,1... | collective-permute-start | bytes 1572872 | tf_op jit(solution)/shard_map/while/body/eval_jaxpr/ppermute | solution.py:13
  722.1 5.4 copy-start.1
  722.2 5.4 copy-start.2
  729.2 14.9 %collective-permute-start = (bf16[128,2048]{1,0:T(8,128)(2,1)S(1)}, bf16[128,2048]{1,0:T(8,128)(2,1)S(1)}, u32[]{:S(2)}, u32[]{:S(2)}) collective-permute-start(bf16[128,2048]{1,0:T(8,128)(2,1)S(1)} %get-tuple-element.220), channel_id=1, source_target_pairs={{0,1},{1,2},{2,3},{3,4},{4,5},{5,6},{6,7},{7,8},{8,9},{9,10},{10,1... | collective-permute-start | bytes 1572872 | tf_op jit(solution)/shard_map/while/body/eval_jaxpr/ppermute | solution.py:13
  745.1 16.1 %collective-permute-start = (bf16[128,2048]{1,0:T(8,128)(2,1)S(1)}, bf16[128,2048]{1,0:T(8,128)(2,1)S(1)}, u32[]{:S(2)}, u32[]{:S(2)}) collective-permute-start(bf16[128,2048]{1,0:T(8,128)(2,1)S(1)} %get-tuple-element.220), channel_id=1, source_target_pairs={{0,1},{1,2},{2,3},{3,4},{4,5},{5,6},{6,7},{7,8},{8,9},{9,10},{10,1... | collective-permute-start | bytes 1572872 | tf_op jit(solution)/shard_map/while/body/eval_jaxpr/ppermute | solution.py:13
  762.1 16.1 %collective-permute-start = (bf16[128,2048]{1,0:T(8,128)(2,1)S(1)}, bf16[128,2048]{1,0:T(8,128)(2,1)S(1)}, u32[]{:S(2)}, u32[]{:S(2)}) collective-permute-start(bf16[128,2048]{1,0:T(8,128)(2,1)S(1)} %get-tuple-element.220), channel_id=1, source_target_pairs={{0,1},{1,2},{2,3},{3,4},{4,5},{5,6},{6,7},{7,8},{8,9},{9,10},{10,1... | collective-permute-start | bytes 1572872 | tf_op jit(solution)/shard_map/while/body/eval_jaxpr/ppermute | solution.py:13
  779.2 15.3 %collective-permute-start = (bf16[128,2048]{1,0:T(8,128)(2,1)S(1)}, bf16[128,2048]{1,0:T(8,128)(2,1)S(1)}, u32[]{:S(2)}, u32[]{:S(2)}) collective-permute-start(bf16[128,2048]{1,0:T(8,128)(2,1)S(1)} %get-tuple-element.220), channel_id=1, source_target_pairs={{0,1},{1,2},{2,3},{3,4},{4,5},{5,6},{6,7},{7,8},{8,9},{9,10},{10,1... | collective-permute-start | bytes 1572872 | tf_op jit(solution)/shard_map/while/body/eval_jaxpr/ppermute | solution.py:13
  795.4 18.2 %collective-permute-start = (bf16[128,2048]{1,0:T(8,128)(2,1)S(1)}, bf16[128,2048]{1,0:T(8,128)(2,1)S(1)}, u32[]{:S(2)}, u32[]{:S(2)}) collective-permute-start(bf16[128,2048]{1,0:T(8,128)(2,1)S(1)} %get-tuple-element.220), channel_id=1, source_target_pairs={{0,1},{1,2},{2,3},{3,4},{4,5},{5,6},{6,7},{7,8},{8,9},{9,10},{10,1... | collective-permute-start | bytes 1572872 | tf_op jit(solution)/shard_map/while/body/eval_jaxpr/ppermute | solution.py:13
  814.4 18.4 %collective-permute-start = (bf16[128,2048]{1,0:T(8,128)(2,1)S(1)}, bf16[128,2048]{1,0:T(8,128)(2,1)S(1)}, u32[]{:S(2)}, u32[]{:S(2)}) collective-permute-start(bf16[128,2048]{1,0:T(8,128)(2,1)S(1)} %get-tuple-element.220), channel_id=1, source_target_pairs={{0,1},{1,2},{2,3},{3,4},{4,5},{5,6},{6,7},{7,8},{8,9},{9,10},{10,1... | collective-permute-start | bytes 1572872 | tf_op jit(solution)/shard_map/while/body/eval_jaxpr/ppermute | solution.py:13
  833.7 17.5 %collective-permute-start = (bf16[128,2048]{1,0:T(8,128)(2,1)S(1)}, bf16[128,2048]{1,0:T(8,128)(2,1)S(1)}, u32[]{:S(2)}, u32[]{:S(2)}) collective-permute-start(bf16[128,2048]{1,0:T(8,128)(2,1)S(1)} %get-tuple-element.220), channel_id=1, source_target_pairs={{0,1},{1,2},{2,3},{3,4},{4,5},{5,6},{6,7},{7,8},{8,9},{9,10},{10,1... | collective-permute-start | bytes 1572872 | tf_op jit(solution)/shard_map/while/body/eval_jaxpr/ppermute | solution.py:13
  852.1 13.8 %collective-permute-start = (bf16[128,2048]{1,0:T(8,128)(2,1)S(1)}, bf16[128,2048]{1,0:T(8,128)(2,1)S(1)}, u32[]{:S(2)}, u32[]{:S(2)}) collective-permute-start(bf16[128,2048]{1,0:T(8,128)(2,1)S(1)} %get-tuple-element.220), channel_id=1, source_target_pairs={{0,1},{1,2},{2,3},{3,4},{4,5},{5,6},{6,7},{7,8},{8,9},{9,10},{10,1... | collective-permute-start | bytes 1572872 | tf_op jit(solution)/shard_map/while/body/eval_jaxpr/ppermute | solution.py:13
  866.8 11.7 slice-start
  873.3 5.2 slice-start.1
  873.3 6.4 copy-start
Sparse Core Ops, SparseCore 0:
  934.7 294.1 all-reduce.5
